TPU v7x, 512 devices: a whole 4x8x8 slice. The times are simulated.
512 devices in a mesh: blk: 64 (over y, z_hi, core), req: 8 (over z_lo, x).
Axes of the slice: x: 4, y: 8, z: 8 (z_hi: 4, z_lo: 2; z = z_hi * 2 + z_lo), core: 2. Of those that a mesh axis runs over, the one named last changes fastest.
Arguments:
- tokens: bfloat16 [8192, 1024], P('blk'), may hold values from -6 to 6
- w_qkv: bfloat16 [1024, 3, 1024], P(None, None, 'req'), may hold values from -0.1875 to 0.1875
- w_out: bfloat16 [1024, 1024], P('req'), may hold values from -0.75 to 0.75
- k_pages: bfloat16 [1280, 128, 1024], P('blk', None, 'req'), may hold values from -512 to 512
- v_pages: bfloat16 [1280, 128, 1024], P('blk', None, 'req'), may hold values from -18 to 18
- page_table: int32 [320, 4], P('blk'), may hold values from 0 to 19, as said below
- cache_lens: int32 [320], P('blk'), may hold values from 1 to 512, as said below
- norm1_gain: float32 [1024], replicated, may hold values from 0.5 to 1.5
- norm1_shift: float32 [1024], replicated, may hold values from -3 to 3
- w_up: bfloat16 [1024, 4096], P(None, 'blk'), may hold values from -0.1875 to 0.1875
- w_down: bfloat16 [4096, 1024], P('blk'), may hold values from -0.1875 to 0.1875
- norm2_gain: float32 [1024], replicated, may hold values from 0.5 to 1.5
- norm2_shift: float32 [1024], replicated, may hold values from -3 to 3
Outputs:
- layer_out: bfloat16 [8192, 1024], P(('blk', 'req'))
Inputs may be any that keep to these rules, and one draw needn't show every extreme that they name: `page_table`: the 5 rows of one request group name every page of that group's pool exactly once. `cache_lens`: every request group has at least one request whose cache is full.
All inputs are finite; a program needn't handle non-finite values.
Results may differ from a plain program's by a relative error of at most 0.02.
Values may be sent and summed in bfloat16 or wider, within the bound.
A program may use at most 64 MiB of HBM per device.

v0:
```python
import jax
import jax.numpy as jnp
from jax import lax
from jax.sharding import PartitionSpec as P

HD = 64
epsilon = 1e-05
masked_score = -1e30


def layer_norm(values, gain_vec, shift_vec):
    center = values - jnp.mean(values, axis=-1, keepdims=True)
    spread = jnp.mean(center * center, axis=-1, keepdims=True)
    return center * lax.rsqrt(spread + epsilon) * gain_vec + shift_vec


def attend(queries, key_new, value_new, key_pool, value_pool, page_map, lengths):
    requests = page_map.shape[0]
    stretch_len = queries.shape[0] - (requests - 1)
    head_count = key_pool.shape[2]
    head_size = key_pool.shape[3]
    key_seq = key_pool[page_map].reshape(requests, -1, head_count, head_size)
    value_seq = value_pool[page_map].reshape(requests, -1, head_count, head_size)
    scale_factor = head_size ** (-0.5)
    key_span = key_seq.shape[1]
    positions = jnp.arange(key_span)
    prompt_query = queries[:stretch_len]
    cache_scores = (
        jnp.einsum("chd,shd->hcs", prompt_query, key_seq[0], preferred_element_type=jnp.float32)
        * scale_factor
    )
    cache_scores = jnp.where(positions[None, None, :] < lengths[0], cache_scores, masked_score)
    stretch_scores = (
        jnp.einsum(
            "chd,jhd->hcj", prompt_query, key_new[:stretch_len], preferred_element_type=jnp.float32
        )
        * scale_factor
    )
    causal = jnp.arange(stretch_len)[:, None] >= jnp.arange(stretch_len)[None, :]
    stretch_scores = jnp.where(causal[None], stretch_scores, masked_score)
    top_score = jnp.maximum(
        jnp.max(cache_scores, -1, keepdims=True), jnp.max(stretch_scores, -1, keepdims=True)
    )
    cache_exp = jnp.exp(cache_scores - top_score)
    stretch_exp = jnp.exp(stretch_scores - top_score)
    exp_total = jnp.sum(cache_exp, -1, keepdims=True) + jnp.sum(stretch_exp, -1, keepdims=True)
    cache_weight = (cache_exp / exp_total).astype(jnp.bfloat16)
    stretch_weight = (stretch_exp / exp_total).astype(jnp.bfloat16)
    prompt_out = jnp.einsum(
        "hcs,shd->chd", cache_weight, value_seq[0], preferred_element_type=jnp.float32
    )
    prompt_out = prompt_out + jnp.einsum(
        "hcj,jhd->chd", stretch_weight, value_new[:stretch_len], preferred_element_type=jnp.float32
    )
    step_query = queries[stretch_len:]
    step_scores = (
        jnp.einsum("rhd,rshd->rhs", step_query, key_seq[1:], preferred_element_type=jnp.float32)
        * scale_factor
    )
    step_scores = jnp.where(
        positions[None, None, :] < lengths[1:, None, None], step_scores, masked_score
    )
    self_score = (
        jnp.einsum(
            "rhd,rhd->rh", step_query, key_new[stretch_len:], preferred_element_type=jnp.float32
        )[..., None]
        * scale_factor
    )
    step_top = jnp.maximum(jnp.max(step_scores, -1, keepdims=True), self_score)
    step_exp = jnp.exp(step_scores - step_top)
    self_exp = jnp.exp(self_score - step_top)
    step_total = jnp.sum(step_exp, -1, keepdims=True) + self_exp
    step_weight = (step_exp / step_total).astype(jnp.bfloat16)
    self_weight = (self_exp / step_total).astype(jnp.bfloat16)
    step_out = jnp.einsum(
        "rhs,rshd->rhd", step_weight, value_seq[1:], preferred_element_type=jnp.float32
    )
    step_out = step_out + self_weight.astype(jnp.float32) * value_new[stretch_len:].astype(
        jnp.float32
    )
    merged = jnp.concatenate([prompt_out, step_out], axis=0)
    return merged.astype(jnp.bfloat16).reshape(queries.shape[0], head_count * head_size)


def on_device(
    tokens,
    w_qkv,
    w_out,
    k_pages,
    v_pages,
    page_table,
    cache_lens,
    norm1_gain,
    norm1_shift,
    w_up,
    w_down,
    norm2_gain,
    norm2_shift,
):
    tok_rows, model_width = tokens.shape
    head_cols = w_qkv.shape[2]
    head_count = head_cols // HD
    projected = jnp.dot(
        tokens, w_qkv.reshape(model_width, 3 * head_cols), preferred_element_type=jnp.float32
    ).astype(jnp.bfloat16)
    projected = projected.reshape(tok_rows, 3, head_count, HD)
    pool_pages = k_pages.shape[0]
    key_pool = k_pages.reshape(pool_pages, k_pages.shape[1], head_count, HD)
    value_pool = v_pages.reshape(pool_pages, v_pages.shape[1], head_count, HD)
    attended = attend(
        projected[:, 0],
        projected[:, 1],
        projected[:, 2],
        key_pool,
        value_pool,
        page_table,
        cache_lens,
    )
    partial_out = jnp.dot(attended, w_out, preferred_element_type=jnp.float32)
    own_rows = tok_rows // lax.axis_size("req")
    row_first = lax.axis_index("req") * own_rows
    summed = lax.psum(partial_out.astype(jnp.bfloat16), "req").astype(jnp.float32)
    head_mixed = lax.dynamic_slice_in_dim(summed, row_first, own_rows, 0)
    residual = lax.dynamic_slice_in_dim(tokens, row_first, own_rows, 0).astype(jnp.float32)
    normed = layer_norm(residual + head_mixed, norm1_gain, norm1_shift).astype(jnp.bfloat16)
    hidden = jax.nn.gelu(
        jnp.dot(
            lax.all_gather(normed, "blk", axis=0, tiled=True),
            w_up,
            preferred_element_type=jnp.float32,
        ),
        approximate=False,
    ).astype(jnp.bfloat16)
    branch = lax.psum_scatter(
        jnp.dot(hidden, w_down, preferred_element_type=jnp.float32),
        "blk",
        scatter_dimension=0,
        tiled=True,
    )
    return layer_norm(normed.astype(jnp.float32) + branch, norm2_gain, norm2_shift).astype(
        jnp.bfloat16
    )


def solution(mesh):
    return jax.shard_map(
        on_device,
        mesh=mesh,
        in_specs=(
            P("blk", None),
            P(None, None, "req"),
            P("req", None),
            P("blk", None, "req"),
            P("blk", None, "req"),
            P("blk", None),
            P("blk"),
            P(),
            P(),
            P(None, "blk"),
            P("blk", None),
            P(),
            P(),
        ),
        out_specs=P(("blk", "req"), None),
        check_vma=False,
    )
```

profile of v0, /device:TPU:2, one launch (start us, length us, event | category | flops | bytes accessed | tf_op | source)
XLA Modules:
  0.0 365.7 jit_solution(5662125291629240805)
XLA Ops:
  6.5 0.0 all-reduce.2.cloned.1.call-start
  6.6 1.5 copy.45
  8.1 1.3 convolution_convert_fusion.1
  9.4 0.1 copy.46
  9.5 0.1 fusion.58
  9.7 0.1 slice_bitcast_fusion.11
  9.7 0.1 slice.78
  9.9 0.1 iota_compare_fusion.1
  9.9 0.1 copy.43
  10.0 0.1 reshape.129
  10.1 0.3 copy.47
  10.5 0.7 gather_fusion.1
  11.2 0.3 copy.50
  11.6 0.2 slice.82
  11.8 0.5 copy-done.3
  12.2 0.3 copy.42
  12.6 0.7 gather_fusion
  13.3 0.3 copy.51
  13.7 0.2 slice.86
  13.9 0.3 fusion.105
  14.2 0.1 copy.53
  14.3 0.2 fusion.5
  14.5 0.1 fusion.71
  14.7 0.2 fusion.69
  14.8 0.1 fusion.70
  14.9 0.2 fusion.3
  15.2 0.1 copy.61
  15.3 0.2 fusion.106
  15.6 0.2 fusion.7
  15.9 0.3 fusion.18
  16.2 0.2 fusion.2
  16.4 0.1 fusion.57
  16.5 1.0 convolution_convert_fusion
  17.5 0.0 all-reduce.2.cloned.1.call-update
  17.5 0.0 all-gather.2.cloned.1.call-start
  17.6 88.0 %all-reduce.2.cloned.1.call-done = bf16[128,1024]{1,0:T(8,128)(2,1)} async-done(((bf16[128,1024]{1,0:T(8,128)(2,1)}), bf16[128,1024]{1,0:T(8,128)(2,1)}) %all-reduce.2.cloned.1.call-update) | async-done | bytes 262160 | tf_op jit(solution)/shard_map/psum | solution.py:122
  105.6 0.9 fusion.62
  106.5 1.0 multiply_reduce_fusion.1
  107.5 1.5 add_convert_fusion.1
  108.9 0.0 all-gather.2.cloned.1.call-update
  109.0 0.0 reduce-scatter.2.cloned.1.call-start
  109.0 86.5 %all-gather.2.cloned.1.call-done = bf16[1024,1024]{1,0:T(8,128)(2,1)} async-done(((bf16[16,1024]{1,0:T(8,128)(2,1)}), bf16[1024,1024]{1,0:T(8,128)(2,1)}) %all-gather.2.cloned.1.call-update) | async-done | bytes 2097168 | tf_op jit(solution)/shard_map/all_gather | solution.py:128
  195.5 5.3 %fusion.19 = f32[1024,1024]{1,0:T(8,128)} fusion(bf16[64,1024]{1,0:T(8,128)(2,1)S(1)} %copy-done.9, bf16[1024,1024]{1,0:T(8,128)(2,1)} %all-gather.2.cloned.1.call-done, bf16[1024,64]{0,1:T(8,128)(2,1)S(1)} %copy-done.10), kind=kOutput, calls=%fused_computation.37 | convolution fusion | flops 272695296 | bytes 6553600 | tf_op jit(solution)/shard_map/dot_general | solution.py:135
  200.8 0.0 reduce-scatter.2.cloned.1.call-update
  200.9 154.7 %reduce-scatter.2.cloned.1.call-done = f32[16,1024]{1,0:T(8,128)} async-done(((f32[1024,1024]{1,0:T(8,128)}), f32[16,1024]{1,0:T(8,128)}) %reduce-scatter.2.cloned.1.call-update) | async-done | bytes 65552 | tf_op jit(solution)/shard_map/reduce_scatter | solution.py:134
  355.6 1.0 fusion.66
  356.6 1.0 multiply_reduce_fusion
  357.6 1.5 add_convert_fusion
  (38 shorter events, 0.3 us)
Async XLA Ops:
  6.5 10.0 %copy-start = (bf16[128,1024]{1,0:T(8,128)(2,1)S(1)}, bf16[128,1024]{1,0:T(8,128)(2,1)}, u32[]{:S(2)}) copy-start(bf16[128,1024]{1,0:T(8,128)(2,1)} %param.15) | copy-start | bytes 786436
  6.5 3.2 copy-start.11
  6.5 3.4 copy-start.8
  6.5 3.6 copy-start.2
  6.5 99.0 %all-reduce.2.cloned.1.call-start = ((), (), s32[]{:S(2)}) async-start(), calls=%async_computation.1 | async-start | bytes 524288 | tf_op jit(solution)/shard_map/psum | solution.py:122
  11.2 1.1 copy-start.3
  15.8 91.6 %copy-start.6 = (f32[1024]{0:T(1024)S(1)}, f32[1024]{0:T(1024)}, u32[]{:S(2)}) copy-start(f32[1024]{0:T(1024)} %param.21) | copy-start | bytes 12292
  15.8 91.6 %copy-start.7 = (f32[1024]{0:T(1024)S(1)}, f32[1024]{0:T(1024)}, u32[]{:S(2)}) copy-start(f32[1024]{0:T(1024)} %param.20) | copy-start | bytes 12292
  15.9 179.6 %copy-start.9 = (bf16[64,1024]{1,0:T(8,128)(2,1)S(1)}, bf16[64,1024]{1,0:T(8,128)(2,1)}, u32[]{:S(2)}) copy-start(bf16[64,1024]{1,0:T(8,128)(2,1)} %param.23) | copy-start | bytes 393220
  15.9 179.6 %copy-start.10 = (bf16[1024,64]{0,1:T(8,128)(2,1)S(1)}, bf16[1024,64]{0,1:T(8,128)(2,1)}, u32[]{:S(2)}) copy-start(bf16[1024,64]{0,1:T(8,128)(2,1)} %param.22) | copy-start | bytes 393220
  17.5 178.0 %all-gather.2.cloned.1.call-start = ((), (), s32[]{:S(2)}) async-start(), calls=%async_computation.2 | async-start | bytes 2129920 | tf_op jit(solution)/shard_map/all_gather | solution.py:128
  109.0 246.6 %reduce-scatter.2.cloned.1.call-start = ((), (), s32[]{:S(2)}) async-start(), calls=%async_computation.3 | async-start | bytes 4259840 | tf_op jit(solution)/shard_map/reduce_scatter | solution.py:134
  200.8 154.8 %copy-start.1 = (bf16[16,1024]{1,0:T(8,128)(2,1)S(1)}, bf16[16,1024]{1,0:T(8,128)(2,1)}, u32[]{:S(2)}) copy-start(bf16[16,1024]{1,0:T(8,128)(2,1)} %add_convert_fusion.1) | copy-start | bytes 98308
  200.8 156.8 %copy-start.4 = (f32[1024]{0:T(1024)S(1)}, f32[1024]{0:T(1024)}, u32[]{:S(2)}) copy-start(f32[1024]{0:T(1024)} %param.25) | copy-start | bytes 12292
  200.8 156.8 %copy-start.5 = (f32[1024]{0:T(1024)S(1)}, f32[1024]{0:T(1024)}, u32[]{:S(2)}) copy-start(f32[1024]{0:T(1024)} %param.24) | copy-start | bytes 12292
Sparse Core Ops, SparseCore 0:
  17.7 87.8 all-reduce.1
  109.1 86.3 all-gather.1
  201.0 154.5 reduce-scatter.1
where the time goes:
time: 366 us
  waiting for transfers between devices  329 us (90%)
  between operations  13.4 us (4%)
  matrix products  9.21 us (3%)
  other arithmetic  7.88 us (2%)
  local copies, waits for them, and re-layouts  5.86 us (2%)
    reduce_scatter x1, waiting for transfers between devices, on_device(): lax.psum_scatter(jnp.dot(hidden, w_down, preferred_element_type=jnp.float...  155 us
    psum x1, waiting for transfers between devices, on_device(): lax.psum(partial_out.astype(jnp.bfloat16), 'req').astype(jnp.float32)  88 us
    all_gather x1, waiting for transfers between devices, on_device(): lax.all_gather(normed, 'blk', axis=0, tiled=True)  86.5 us
  transfers between devices with their start and end apart: 3, of which 3 were waited for; matrix products, arithmetic and copies ran while one was open for 0% of the time, Pallas kernels for 0%

commit v1 on v0

--- a/solution.py
+++ b/solution.py
@@ -125,7 +125,9 @@
     normed = layer_norm(residual + head_mixed, norm1_gain, norm1_shift).astype(jnp.bfloat16)
     hidden = jax.nn.gelu(
         jnp.dot(
-            lax.all_gather(normed, "blk", axis=0, tiled=True),
+            jnp.concatenate(
+                lax.all_to_all(jnp.stack([normed] * lax.axis_size("blk")), "blk", 0, 0), axis=0
+            ),
             w_up,
             preferred_element_type=jnp.float32,
         ),

time: 366 us -> 344 us (0.940)
  waiting for transfers between devices: 329 us -> 245 us
  blocking collectives: 0 us -> 63.7 us
    all_gather x1 -> x0, waiting for transfers between devices: 86.5 us -> none  [on_device(): lax.all_gather(normed, 'blk', axis=0, tiled=True)]
    all_to_all x0 -> x1, blocking collectives: none -> 63.7 us  [on_device(): lax.all_to_all(jnp.stack([normed] * lax.axis_size('blk')), 'blk', 0, 0)]
  transfers between devices with their start and end apart: 3 -> 2, of which waited for: 3 -> 2; matrix products, arithmetic and copies ran while one was open for 0% -> 0% of each run, Pallas kernels for 0% -> 0%
where the time goes in v1:
time: 344 us
  waiting for transfers between devices  245 us (71%)
  blocking collectives  63.7 us (19%)
  between operations  13.7 us (4%)
  matrix products  7.61 us (2%)
  other arithmetic  7.27 us (2%)
  local copies, waits for them, and re-layouts  6.11 us (2%)
    reduce_scatter x1, waiting for transfers between devices, on_device(): lax.psum_scatter(jnp.dot(hidden, w_down, preferred_element_type=jnp.float...  157 us
    psum x1, waiting for transfers between devices, on_device(): lax.psum(partial_out.astype(jnp.bfloat16), 'req').astype(jnp.float32)  88 us
    all_to_all x1, blocking collectives, on_device(): lax.all_to_all(jnp.stack([normed] * lax.axis_size('blk')), 'blk', 0, 0)  63.7 us
  transfers between devices with their start and end apart: 2, of which 2 were waited for; matrix products, arithmetic and copies ran while one was open for 0% of the time, Pallas kernels for 0%

profile of v1, /device:TPU:2, one launch (start us, length us, event | category | flops | bytes accessed | tf_op | source)
XLA Modules:
  0.0 343.5 jit_solution(15234300271910574095)
XLA Ops:
  6.5 0.0 all-reduce.2.cloned.1.call-start
  6.6 1.5 copy.45
  8.1 1.3 convolution_convert_fusion.1
  9.4 0.1 copy.46
  9.5 0.1 fusion.58
  9.7 0.1 slice_bitcast_fusion.11
  9.7 0.1 slice.78
  9.9 0.1 iota_compare_fusion.1
  9.9 0.1 copy.43
  10.0 0.1 reshape.135
  10.1 0.3 copy.47
  10.5 0.7 gather_fusion.1
  11.2 0.3 copy.50
  11.6 0.2 slice.82
  11.8 0.5 copy-done.2
  12.2 0.3 copy.42
  12.6 0.7 gather_fusion
  13.3 0.3 copy.51
  13.7 0.2 slice.86
  13.9 0.3 fusion.105
  14.2 0.1 copy.53
  14.3 0.2 fusion.5
  14.5 0.1 fusion.71
  14.7 0.2 fusion.69
  14.8 0.1 fusion.70
  14.9 0.2 fusion.3
  15.2 0.1 copy.61
  15.3 0.2 fusion.106
  15.6 0.2 fusion.7
  15.9 0.3 fusion.18
  16.2 0.2 fusion.2
  16.4 0.1 fusion.57
  16.5 1.0 convolution_convert_fusion
  17.5 0.0 all-reduce.2.cloned.1.call-update
  17.5 0.0 reduce-scatter.2.cloned.1.call-start
  17.6 88.0 %all-reduce.2.cloned.1.call-done = bf16[128,1024]{1,0:T(8,128)(2,1)} async-done(((bf16[128,1024]{1,0:T(8,128)(2,1)}), bf16[128,1024]{1,0:T(8,128)(2,1)}) %all-reduce.2.cloned.1.call-update) | async-done | bytes 262160 | tf_op jit(solution)/shard_map/psum | solution.py:122
  105.5 0.9 fusion.62
  106.4 1.0 multiply_reduce_fusion.1
  107.4 0.9 add_convert_fusion.1
  108.3 0.2 stack.2
  108.5 0.0 copy-start.8
  108.6 63.7 %all_to_all.5 = bf16[64,16,1024]{2,1,0:T(8,128)(2,1)S(1)} all-to-all(bf16[64,16,1024]{2,1,0:T(8,128)(2,1)S(1)} %stack.2), channel_id=1, replica_groups=mesh['blk'=64,'req'=8] {'blk'}, dimensions={0} | all-to-all | bytes 4194304 | tf_op jit(solution)/shard_map/all_to_all | solution.py:129
  172.3 3.7 %fusion.19 = f32[1024,1024]{1,0:T(8,128)} fusion(bf16[64,1024]{1,0:T(8,128)(2,1)S(1)} %copy-done.8, bf16[1024,1024]{1,0:T(8,128)(2,1)S(1)} %bitcast.88, bf16[1024,64]{0,1:T(8,128)(2,1)S(1)} %copy-done.9), kind=kOutput, calls=%fused_computation.37 | convolution fusion | flops 272695296 | bytes 6553600 | tf_op jit(solution)/shard_map/dot_general | solution.py:137
  176.1 0.0 reduce-scatter.2.cloned.1.call-update
  176.1 157.1 %reduce-scatter.2.cloned.1.call-done = f32[16,1024]{1,0:T(8,128)} async-done(((f32[1024,1024]{1,0:T(8,128)}), f32[16,1024]{1,0:T(8,128)}) %reduce-scatter.2.cloned.1.call-update) | async-done | bytes 65552 | tf_op jit(solution)/shard_map/reduce_scatter | solution.py:136
  333.1 1.0 fusion.66
  334.1 1.0 multiply_reduce_fusion
  335.2 1.5 add_convert_fusion
  (35 shorter events, 0.3 us)
Async XLA Ops:
  6.5 9.9 %copy-start = (bf16[128,1024]{1,0:T(8,128)(2,1)S(1)}, bf16[128,1024]{1,0:T(8,128)(2,1)}, u32[]{:S(2)}) copy-start(bf16[128,1024]{1,0:T(8,128)(2,1)} %param.15) | copy-start | bytes 786436
  6.5 3.2 copy-start.10
  6.5 3.4 copy-start.7
  6.5 3.6 %copy-start.1 = (bf16[20,128,128]{2,1,0:T(8,128)(2,1)S(1)}, bf16[20,128,128]{2,1,0:T(8,128)(2,1)}, u32[]{:S(2)}) copy-start(bf16[20,128,128]{2,1,0:T(8,128)(2,1)} %param.16) | copy-start | bytes 1966084
  6.5 99.0 %all-reduce.2.cloned.1.call-start = ((), (), s32[]{:S(2)}) async-start(), calls=%async_computation.2 | async-start | bytes 524288 | tf_op jit(solution)/shard_map/psum | solution.py:122
  11.2 1.1 copy-start.2
  15.8 91.6 %copy-start.5 = (f32[1024]{0:T(1024)S(1)}, f32[1024]{0:T(1024)}, u32[]{:S(2)}) copy-start(f32[1024]{0:T(1024)} %param.21) | copy-start | bytes 12292
  15.8 91.6 %copy-start.6 = (f32[1024]{0:T(1024)S(1)}, f32[1024]{0:T(1024)}, u32[]{:S(2)}) copy-start(f32[1024]{0:T(1024)} %param.20) | copy-start | bytes 12292
  17.5 315.6 %reduce-scatter.2.cloned.1.call-start = ((), (), s32[]{:S(2)}) async-start(), calls=%async_computation.3 | async-start | bytes 4259840 | tf_op jit(solution)/shard_map/reduce_scatter | solution.py:136
  108.5 63.8 %copy-start.8 = (bf16[64,1024]{1,0:T(8,128)(2,1)S(1)}, bf16[64,1024]{1,0:T(8,128)(2,1)}, u32[]{:S(2)}) copy-start(bf16[64,1024]{1,0:T(8,128)(2,1)} %param.23) | copy-start | bytes 393220
  108.6 63.8 %copy-start.9 = (bf16[1024,64]{0,1:T(8,128)(2,1)S(1)}, bf16[1024,64]{0,1:T(8,128)(2,1)}, u32[]{:S(2)}) copy-start(bf16[1024,64]{0,1:T(8,128)(2,1)} %param.22) | copy-start | bytes 393220
  176.0 159.1 %copy-start.3 = (f32[1024]{0:T(1024)S(1)}, f32[1024]{0:T(1024)}, u32[]{:S(2)}) copy-start(f32[1024]{0:T(1024)} %param.25) | copy-start | bytes 12292
  176.1 159.1 %copy-start.4 = (f32[1024]{0:T(1024)S(1)}, f32[1024]{0:T(1024)}, u32[]{:S(2)}) copy-start(f32[1024]{0:T(1024)} %param.24) | copy-start | bytes 12292
Sparse Core Ops, SparseCore 0:
  17.6 87.8 all-reduce.1
  176.2 156.8 reduce-scatter.1

commit v2 on v0

--- a/solution.py
+++ b/solution.py
@@ -119,7 +119,9 @@
     partial_out = jnp.dot(attended, w_out, preferred_element_type=jnp.float32)
     own_rows = tok_rows // lax.axis_size("req")
     row_first = lax.axis_index("req") * own_rows
-    summed = lax.psum(partial_out.astype(jnp.bfloat16), "req").astype(jnp.float32)
+    summed = jnp.sum(lax.all_gather(partial_out.astype(jnp.bfloat16), "req"), axis=0).astype(
+        jnp.float32
+    )
     head_mixed = lax.dynamic_slice_in_dim(summed, row_first, own_rows, 0)
     residual = lax.dynamic_slice_in_dim(tokens, row_first, own_rows, 0).astype(jnp.float32)
     normed = layer_norm(residual + head_mixed, norm1_gain, norm1_shift).astype(jnp.bfloat16)

time: 366 us -> 330 us (0.902)
  waiting for transfers between devices: 329 us -> 291 us
    psum x1 -> x0, waiting for transfers between devices: 88 us -> none  [on_device(): lax.psum(partial_out.astype(jnp.bfloat16), 'req').astype(jnp.float32)]
    all_gather x0 -> x1, waiting for transfers between devices: none -> 49.1 us  [on_device(): lax.all_gather(partial_out.astype(jnp.bfloat16), 'req')]
where the time goes in v2:
time: 330 us; the launch traced here: 329 us
  waiting for transfers between devices  291 us (88%)
  between operations  13.4 us (4%)
  other arithmetic  9.81 us (3%)
  matrix products  9.25 us (3%)
  local copies, waits for them, and re-layouts  5.86 us (2%)
    reduce_scatter x1, waiting for transfers between devices, on_device(): lax.psum_scatter(jnp.dot(hidden, w_down, preferred_element_type=jnp.float...  155 us
    all_gather x1, waiting for transfers between devices, on_device(): lax.all_gather(normed, 'blk', axis=0, tiled=True)  86.7 us
    all_gather x1, waiting for transfers between devices, on_device(): lax.all_gather(partial_out.astype(jnp.bfloat16), 'req')  49.1 us
  transfers between devices with their start and end apart: 3, of which 3 were waited for; matrix products, arithmetic and copies ran while one was open for 0% of the time, Pallas kernels for 0%

profile of v2, /device:TPU:2, one launch (start us, length us, event | category | flops | bytes accessed | tf_op | source)
XLA Modules:
  0.0 329.0 jit_solution(434383866190343432)
XLA Ops:
  6.5 0.0 all-gather.6.cloned.1.call-start
  6.6 1.5 copy.45
  8.1 1.3 convolution_convert_fusion.1
  9.4 0.1 copy.46
  9.5 0.1 fusion.58
  9.7 0.1 slice_bitcast_fusion.11
  9.7 0.1 slice.78
  9.9 0.1 iota_compare_fusion.1
  9.9 0.1 copy.43
  10.0 0.1 reshape.129
  10.1 0.3 copy.47
  10.5 0.7 gather_fusion.1
  11.2 0.3 copy.50
  11.6 0.2 slice.82
  11.8 0.5 copy-done.3
  12.2 0.3 copy.42
  12.6 0.7 gather_fusion
  13.3 0.3 copy.51
  13.7 0.2 slice.86
  13.9 0.3 fusion.105
  14.2 0.1 copy.53
  14.3 0.2 fusion.5
  14.5 0.1 fusion.71
  14.7 0.2 fusion.69
  14.8 0.1 fusion.70
  14.9 0.2 fusion.3
  15.2 0.1 copy.61
  15.3 0.2 fusion.106
  15.6 0.2 fusion.7
  15.8 0.3 fusion.18
  16.2 0.2 fusion.2
  16.4 0.1 fusion.57
  16.5 1.1 convolution_convert_fusion
  17.6 0.0 all-gather.6.cloned.1.call-update
  17.6 0.0 all-gather.4.cloned.1.call-start
  17.6 49.1 %all-gather.6.cloned.1.call-done = bf16[1024,1024]{1,0:T(8,128)(2,1)} async-done(((bf16[128,1024]{1,0:T(8,128)(2,1)}), bf16[1024,1024]{1,0:T(8,128)(2,1)}) %all-gather.6.cloned.1.call-update) | async-done | bytes 2097168 | tf_op jit(solution)/shard_map/all_gather | solution.py:122
  66.7 2.0 reduce_sum.78
  68.7 0.9 fusion.62
  69.6 1.0 multiply_reduce_fusion.1
  70.5 1.5 add_convert_fusion.1
  72.0 0.0 reduce-scatter.2.cloned.1.call-start
  72.1 86.7 %all-gather.4.cloned.1.call-done = bf16[1024,1024]{1,0:T(8,128)(2,1)} async-done(((bf16[16,1024]{1,0:T(8,128)(2,1)}), bf16[1024,1024]{1,0:T(8,128)(2,1)}) %all-gather.4.cloned.1.call-update) | async-done | bytes 2097168 | tf_op jit(solution)/shard_map/all_gather | solution.py:130
  158.8 5.3 %fusion.19 = f32[1024,1024]{1,0:T(8,128)} fusion(bf16[64,1024]{1,0:T(8,128)(2,1)S(1)} %copy-done.9, bf16[1024,1024]{1,0:T(8,128)(2,1)} %all-gather.4.cloned.1.call-done, bf16[1024,64]{0,1:T(8,128)(2,1)S(1)} %copy-done.10), kind=kOutput, calls=%fused_computation.37 | convolution fusion | flops 272695296 | bytes 6553600 | tf_op jit(solution)/shard_map/dot_general | solution.py:137
  164.1 0.0 reduce-scatter.2.cloned.1.call-update
  164.1 154.8 %reduce-scatter.2.cloned.1.call-done = f32[16,1024]{1,0:T(8,128)} async-done(((f32[1024,1024]{1,0:T(8,128)}), f32[16,1024]{1,0:T(8,128)}) %reduce-scatter.2.cloned.1.call-update) | async-done | bytes 65552 | tf_op jit(solution)/shard_map/reduce_scatter | solution.py:136
  318.9 1.0 fusion.66
  319.9 1.0 multiply_reduce_fusion
  320.9 1.5 add_convert_fusion
  (39 shorter events, 0.3 us)
Async XLA Ops:
  6.5 10.0 %copy-start = (bf16[128,1024]{1,0:T(8,128)(2,1)S(1)}, bf16[128,1024]{1,0:T(8,128)(2,1)}, u32[]{:S(2)}) copy-start(bf16[128,1024]{1,0:T(8,128)(2,1)} %param.15) | copy-start | bytes 786436
  6.5 3.2 copy-start.11
  6.5 3.4 %copy-start.8 = (s32[5,4]{0,1:T(4,128)S(1)}, s32[5,4]{0,1:T(4,128)}, u32[]{:S(2)}) copy-start(s32[5,4]{0,1:T(4,128)} %param.18) | copy-start | bytes 244
  6.5 3.6 %copy-start.2 = (bf16[20,128,128]{2,1,0:T(8,128)(2,1)S(1)}, bf16[20,128,128]{2,1,0:T(8,128)(2,1)}, u32[]{:S(2)}) copy-start(bf16[20,128,128]{2,1,0:T(8,128)(2,1)} %param.16) | copy-start | bytes 1966084
  6.5 60.2 %all-gather.6.cloned.1.call-start = ((), (), s32[]{:S(2)}) async-start(), calls=%async_computation.3 | async-start | bytes 2359296 | tf_op jit(solution)/shard_map/all_gather | solution.py:122
  11.2 1.1 copy-start.3
  16.2 54.3 %copy-start.6 = (f32[1024]{0:T(1024)S(1)}, f32[1024]{0:T(1024)}, u32[]{:S(2)}) copy-start(f32[1024]{0:T(1024)} %param.21) | copy-start | bytes 12292
  16.2 54.3 %copy-start.7 = (f32[1024]{0:T(1024)S(1)}, f32[1024]{0:T(1024)}, u32[]{:S(2)}) copy-start(f32[1024]{0:T(1024)} %param.20) | copy-start | bytes 12292
  16.2 142.6 %copy-start.9 = (bf16[64,1024]{1,0:T(8,128)(2,1)S(1)}, bf16[64,1024]{1,0:T(8,128)(2,1)}, u32[]{:S(2)}) copy-start(bf16[64,1024]{1,0:T(8,128)(2,1)} %param.23) | copy-start | bytes 393220
  16.2 142.6 %copy-start.10 = (bf16[1024,64]{0,1:T(8,128)(2,1)S(1)}, bf16[1024,64]{0,1:T(8,128)(2,1)}, u32[]{:S(2)}) copy-start(bf16[1024,64]{0,1:T(8,128)(2,1)} %param.22) | copy-start | bytes 393220
  17.6 141.2 %all-gather.4.cloned.1.call-start = ((), (), s32[]{:S(2)}) async-start(), calls=%async_computation.1 | async-start | bytes 2129920 | tf_op jit(solution)/shard_map/all_gather | solution.py:130
  72.0 246.9 %reduce-scatter.2.cloned.1.call-start = ((), (), s32[]{:S(2)}) async-start(), calls=%async_computation.2 | async-start | bytes 4259840 | tf_op jit(solution)/shard_map/reduce_scatter | solution.py:136
  164.1 154.8 %copy-start.1 = (bf16[16,1024]{1,0:T(8,128)(2,1)S(1)}, bf16[16,1024]{1,0:T(8,128)(2,1)}, u32[]{:S(2)}) copy-start(bf16[16,1024]{1,0:T(8,128)(2,1)} %add_convert_fusion.1) | copy-start | bytes 98308
  164.1 156.8 %copy-start.4 = (f32[1024]{0:T(1024)S(1)}, f32[1024]{0:T(1024)}, u32[]{:S(2)}) copy-start(f32[1024]{0:T(1024)} %param.25) | copy-start | bytes 12292
  164.1 156.8 %copy-start.5 = (f32[1024]{0:T(1024)S(1)}, f32[1024]{0:T(1024)}, u32[]{:S(2)}) copy-start(f32[1024]{0:T(1024)} %param.24) | copy-start | bytes 12292
Sparse Core Ops, SparseCore 0:
  17.7 48.9 all-gather.5
  72.1 86.5 all-gather.3
  164.3 154.5 reduce-scatter.1
